TPU v7x, 256 devices: a whole 4x4x8 slice. The times are simulated.
256 devices in a mesh: dp: 2 (over y_hi), fsdp: 16 (over x, y_lo, core), tensor: 8 (over z).
Axes of the slice: x: 4, y: 4 (y_hi: 2, y_lo: 2; y = y_hi * 2 + y_lo), z: 8, core: 2. Of those that a mesh axis runs over, the one named last changes fastest.
Arguments:
- activations: bfloat16 [4096, 8192], P(('dp', 'fsdp'), 'tensor'), may hold values from -6 to 6
- cotangent: bfloat16 [4096, 8192], P(('dp', 'fsdp'), 'tensor'), may hold values from -6 to 6
- up_tiles: bfloat16 [1024, 128, 128], P(('fsdp', 'tensor')), may hold values from -0.1875 to 0.1875
- down_tiles: bfloat16 [1024, 128, 128], P(('fsdp', 'tensor')), may hold values from -0.125 to 0.125
- up_rows: int32 [128, 8], P(None, 'tensor'), may hold values from 0 to 63, as said below
- up_cols: int32 [128, 8], P(None, 'tensor'), may hold values from 0 to 15, as said below
- down_rows: int32 [128, 8], P(None, 'tensor'), may hold values from 0 to 15, as said below
- down_cols: int32 [128, 8], P(None, 'tensor'), may hold values from 0 to 63, as said below
Outputs:
- output: bfloat16 [4096, 8192], P(('dp', 'fsdp'), 'tensor')
- input_grad: bfloat16 [4096, 8192], P(('dp', 'fsdp'), 'tensor')
- up_grad: float32 [1024, 128, 128], P(('fsdp', 'tensor'))
- down_grad: float32 [1024, 128, 128], P(('fsdp', 'tensor'))
Inputs may be any that keep to these rules, and one draw needn't show every extreme that they name: `up_rows`: within a column, the up tiles of one hidden-unit block name distinct feature blocks. `up_cols`: every value occurs exactly 8 times in each column. `down_rows`: every value occurs exactly 8 times in each column. `down_cols`: within a column, the down tiles of one hidden-unit block name distinct feature blocks.
All inputs are finite; a program needn't handle non-finite values.
Results may differ from a plain program's by a relative error of at most 0.018.
Values may be sent and summed in bfloat16 or wider, within the bound.
No kernel may reach another device: no remote copies, remote signals or barrier semaphores. Data moves between devices by JAX's collectives and lax.ppermute only.
A program may use at most 128 MiB of HBM per device.

v0:
```python
import jax
import jax.numpy as jnp
from jax import lax
from jax.sharding import PartitionSpec as P

D = 8192
FF = 16384
inv_root_two = 0.7071067811865476
inv_root_tau = 0.3989422804014327


def gelu_parts(values):
    normal_cdf = 0.5 * (1.0 + jax.scipy.special.erf(values * inv_root_two))
    density = inv_root_tau * jnp.exp(-0.5 * values * values)
    return (values * normal_cdf, normal_cdf + values * density)


def grouped_pick(acting, far_index, hidden_blocks, block_size):
    rows_here = acting.shape[0]
    picked = acting.reshape(rows_here, -1, block_size)[:, far_index]
    return picked.reshape(rows_here, hidden_blocks, -1, block_size)


def add_far(product, far_index, model_blocks):
    rows_here = product.shape[0]
    block_size = product.shape[-1]
    flat = product.reshape(rows_here, -1, block_size)
    summed = (
        jnp.zeros((rows_here, model_blocks, block_size), jnp.float32).at[:, far_index].add(flat)
    )
    return summed.reshape(rows_here, model_blocks * block_size)


def grouped_tiles(tiles, order, hidden_blocks):
    block_size = tiles.shape[1]
    return tiles[order].reshape(hidden_blocks, -1, block_size, block_size)


def body(activations, cotangent, up_tiles, down_tiles, up_rows, up_cols, down_rows, down_cols):
    block_size = up_tiles.shape[1]
    hidden_blocks = FF // (block_size * lax.axis_size("tensor"))
    model_blocks = D // block_size
    up_order = jnp.argsort(up_cols[:, 0], stable=True)
    down_order = jnp.argsort(down_rows[:, 0], stable=True)
    up_back = jnp.argsort(up_order)
    down_back = jnp.argsort(down_order)
    up_far = up_rows[:, 0][up_order]
    down_far = down_cols[:, 0][down_order]
    full_input = lax.all_gather(activations, "tensor", axis=1, tiled=True)
    input_pick = grouped_pick(full_input, up_far, hidden_blocks, block_size)
    up_whole = lax.all_gather(up_tiles, "fsdp", axis=0, tiled=True)
    up_sorted = grouped_tiles(up_whole, up_order, hidden_blocks)
    pre_act = jnp.einsum(
        "thkb,hkbc->thc", input_pick, up_sorted, preferred_element_type=jnp.float32
    )
    gelu_out, gelu_slope = gelu_parts(pre_act)
    hidden = gelu_out.astype(jnp.bfloat16)
    down_whole = lax.all_gather(down_tiles, "fsdp", axis=0, tiled=True)
    down_sorted = grouped_tiles(down_whole, down_order, hidden_blocks)
    out_product = jnp.einsum(
        "thb,hkbc->thkc", hidden, down_sorted, preferred_element_type=jnp.float32
    )
    partial_out = add_far(out_product, down_far, model_blocks)
    output = lax.psum_scatter(
        partial_out.astype(jnp.bfloat16), "tensor", scatter_dimension=1, tiled=True
    )
    full_cotangent = lax.all_gather(cotangent, "tensor", axis=1, tiled=True)
    cot_pick = grouped_pick(full_cotangent, down_far, hidden_blocks, block_size)
    hidden_grad = jnp.einsum(
        "thkc,hkbc->thb", cot_pick, down_sorted, preferred_element_type=jnp.float32
    )
    pre_grad = (hidden_grad * gelu_slope).astype(jnp.bfloat16)
    in_product = jnp.einsum(
        "thc,hkbc->thkb", pre_grad, up_sorted, preferred_element_type=jnp.float32
    )
    partial_in = add_far(in_product, up_far, model_blocks)
    input_grad = lax.psum_scatter(
        partial_in.astype(jnp.bfloat16), "tensor", scatter_dimension=1, tiled=True
    )
    up_grouped = jnp.einsum(
        "thkb,thc->hkbc", input_pick, pre_grad, preferred_element_type=jnp.float32
    )
    down_grouped = jnp.einsum(
        "thb,thkc->hkbc", hidden, cot_pick, preferred_element_type=jnp.float32
    )
    up_rounded = up_grouped.astype(jnp.bfloat16).reshape(-1, block_size, block_size)
    down_rounded = down_grouped.astype(jnp.bfloat16).reshape(-1, block_size, block_size)
    up_term = up_rounded[up_back].astype(jnp.float32)
    down_term = down_rounded[down_back].astype(jnp.float32)
    up_part, down_part = (
        lax.psum_scatter(
            up_term.astype(jnp.bfloat16), "fsdp", scatter_dimension=0, tiled=True
        ).astype(jnp.float32),
        lax.psum_scatter(
            down_term.astype(jnp.bfloat16), "fsdp", scatter_dimension=0, tiled=True
        ).astype(jnp.float32),
    )
    up_grad, down_grad = (
        lax.psum(up_part.astype(jnp.bfloat16), "dp").astype(jnp.float32),
        lax.psum(down_part.astype(jnp.bfloat16), "dp").astype(jnp.float32),
    )
    return (output, input_grad, up_grad, down_grad)


def solution(mesh):
    in_specs = (
        P(("dp", "fsdp"), "tensor"),
        P(("dp", "fsdp"), "tensor"),
        P(("fsdp", "tensor"), None, None),
        P(("fsdp", "tensor"), None, None),
        P(None, "tensor"),
        P(None, "tensor"),
        P(None, "tensor"),
        P(None, "tensor"),
    )
    out_specs = (
        P(("dp", "fsdp"), "tensor"),
        P(("dp", "fsdp"), "tensor"),
        P(("fsdp", "tensor"), None, None),
        P(("fsdp", "tensor"), None, None),
    )
    return jax.shard_map(body, mesh=mesh, in_specs=in_specs, out_specs=out_specs, check_vma=False)
```

profile of v0, /device:TPU:1, one launch (start us, length us, event | category | flops | bytes accessed | tf_op | source)
XLA Modules:
  0.0 480.6 jit_solution(9236470539080875752)
XLA Ops:
  24.1 28.0 %all-gather.9.cloned.1.call-done = bf16[128,8192]{0,1:T(8,128)(2,1)} async-done(((bf16[128,1024]{0,1:T(8,128)(2,1)}), bf16[128,8192]{0,1:T(8,128)(2,1)}) %all-gather.9.cloned.1.call-update) | async-done | bytes 2097168 | tf_op jit(solution)/shard_map/all_gather | solution.py:49
  55.3 39.0 %all-gather.11.cloned.1.call-done = bf16[128,8192]{0,1:T(8,128)(2,1)} async-done(((bf16[128,1024]{0,1:T(8,128)(2,1)}), bf16[128,8192]{0,1:T(8,128)(2,1)}) %all-gather.11.cloned.1.call-update) | async-done | bytes 2097168 | tf_op jit(solution)/shard_map/all_gather | solution.py:67
  94.3 4.1 copy.66
  101.4 4.6 gather_fusion.5
  106.0 32.7 %all-gather.7.cloned.1.call-done = bf16[128,128,128]{2,1,0:T(8,128)(2,1)} async-done(((bf16[8,128,128]{2,1,0:T(8,128)(2,1)}), bf16[128,128,128]{2,1,0:T(8,128)(2,1)}) %all-gather.7.cloned.1.call-update) | async-done | bytes 4194320 | tf_op jit(solution)/shard_map/all_gather | solution.py:51
  138.7 5.2 %gather_fusion.2 = bf16[128,128,128]{2,1,0:T(8,128)(2,1)} fusion(bf16[128,128,128]{2,1,0:T(8,128)(2,1)} %all-gather.7.cloned.1.call-done, s32[1024]{0:T(1024)S(1)} %pad_clamp_fusion.4), kind=kCustom, calls=%fused_computation.2 | custom fusion | bytes 8389120 | tf_op jit(solution)/shard_map/gather | solution.py:36
  143.9 4.8 convolution_bitcast_fusion.1
  148.7 31.7 %all-gather.5.cloned.1.call-done = bf16[128,128,128]{2,1,0:T(8,128)(2,1)} async-done(((bf16[8,128,128]{2,1,0:T(8,128)(2,1)}), bf16[128,128,128]{2,1,0:T(8,128)(2,1)}) %all-gather.5.cloned.1.call-update) | async-done | bytes 4194320 | tf_op jit(solution)/shard_map/all_gather | solution.py:58
  180.5 5.2 %gather_fusion.1 = bf16[128,128,128]{2,1,0:T(8,128)(2,1)} fusion(bf16[128,128,128]{2,1,0:T(8,128)(2,1)} %all-gather.5.cloned.1.call-done, s32[1024]{0:T(1024)S(1)} %pad_clamp_fusion.5), kind=kCustom, calls=%fused_computation.1 | custom fusion | bytes 8389120 | tf_op jit(solution)/shard_map/gather | solution.py:36
  185.7 5.0 %fusion.2 = bf16[128,16,128,1]{0,2,3,1:T(8,128)(2,1)S(1)} fusion(bf16[16,8,128,128]{3,2,1,0:T(8,128)(2,1)} %bitcast.84, bf16[128,16,8,128]{3,0,2,1:T(8,128)(2,1)} %bitcast.86, f32[128,16,128]{0,2,1:T(8,128)S(1)} %convolution_bitcast_fusion.1), kind=kOutput, calls=%fused_computation.17 | convolution fusion | flops 539492352 | bytes 9961472 | tf_op jit(solution)/shard_map/thkc,hkbc->thb/dot_general | solution.py:69
  194.0 5.2 %gather_fusion.6 = bf16[128,128,128]{2,1,0:T(8,128)(2,1)} fusion(bf16[128,128,128]{2,1,0:T(8,128)(2,1)} %bitcast.88, s32[1024]{0:T(1024)S(1)} %pad_clamp_fusion.1), kind=kCustom, calls=%fused_computation.6 | custom fusion | bytes 8389120 | tf_op jit(solution)/shard_map/gather | solution.py:88
  202.0 5.6 %convolution_convert_fusion = bf16[16,8,128,128]{3,2,1,0:T(8,128)(2,1)} fusion(bf16[128,16,8,128]{3,0,2,1:T(8,128)(2,1)} %bitcast.87, f32[128,16,128]{0,2,1:T(8,128)S(1)} %convolution_bitcast_fusion.1), kind=kOutput, calls=%fused_computation.10 | convolution fusion | flops 540278784 | bytes 9437184 | tf_op jit(solution)/shard_map/thb,thkc->hkbc/dot_general | solution.py:83
  207.6 6.4 %copy.74 = bf16[128,128,128]{2,1,0:T(8,128)(2,1)} copy(bf16[128,128,128]{1,2,0:T(8,128)(2,1)} %bitcast.89) | data formatting | bytes 8388608 | tf_op jit(solution)/shard_map/reshape | solution.py:87
  214.0 5.3 %gather_fusion.7 = bf16[128,128,128]{2,1,0:T(8,128)(2,1)} fusion(bf16[128,128,128]{2,1,0:T(8,128)(2,1)} %copy.74, s32[1024]{0:T(1024)S(1)} %pad_clamp_fusion), kind=kCustom, calls=%fused_computation.7 | custom fusion | bytes 8389120 | tf_op jit(solution)/shard_map/gather | solution.py:89
  219.4 6.7 %fusion.13 = f32[16,8,128,128]{3,2,1,0:T(8,128)} fusion(bf16[16,8,128,128]{3,2,1,0:T(8,128)(2,1)} %bitcast.77, bf16[128,16,128,1]{0,2,3,1:T(8,128)(2,1)S(1)} %fusion.2), kind=kOutput, calls=%fused_computation.40 | convolution fusion | flops 536870912 | bytes 13107200 | tf_op jit(solution)/shard_map/thc,hkbc->thkb/dot_general | solution.py:73
  226.1 9.0 %copy.68 = f32[128,128,128]{2,0,1:T(8,128)} copy(f32[128,128,128]{0,2,1:T(8,128)} %bitcast.82) | data formatting | bytes 16777216 | tf_op jit(solution)/shard_map/reshape | solution.py:27
  237.6 26.7 %scatter_fusion.1 = f32[128,64,128]{2,0,1:T(8,128)} fusion(f32[128,64,128]{2,0,1:T(8,128)} %broadcast.42.clone.1, s32[128]{0:T(128)S(1)} %fusion.9, f32[128,128,128]{2,1,0:T(8,128)} %bitcast.81), kind=kCustom, calls=%fused_computation.9 | custom fusion | flops 2097152 | bytes 25166336 | tf_op jit(solution)/shard_map/scatter-add | solution.py:29
  270.0 6.8 %fusion.11 = f32[16,8,128,128]{3,2,1,0:T(8,128)} fusion(bf16[16,8,128,128]{3,2,1,0:T(8,128)(2,1)} %bitcast.85, f32[128,16,128]{0,2,1:T(8,128)S(1)} %convolution_bitcast_fusion.1), kind=kOutput, calls=%fused_computation.39 | convolution fusion | flops 538181632 | bytes 13631488 | tf_op jit(solution)/shard_map/thb,hkbc->thkc/dot_general | solution.py:60
  276.7 9.0 %copy.63 = f32[128,128,128]{2,0,1:T(8,128)} copy(f32[128,128,128]{0,2,1:T(8,128)} %bitcast.83) | data formatting | bytes 16777216 | tf_op jit(solution)/shard_map/reshape | solution.py:27
  288.2 26.9 %scatter_fusion = f32[128,64,128]{2,0,1:T(8,128)} fusion(f32[128,64,128]{2,0,1:T(8,128)} %broadcast.42.clone, s32[128]{0:T(128)S(1)} %fusion.8, f32[128,128,128]{2,1,0:T(8,128)} %bitcast.80), kind=kCustom, calls=%fused_computation.8 | custom fusion | flops 2097152 | bytes 25166336 | tf_op jit(solution)/shard_map/scatter-add | solution.py:29
  320.7 16.4 %reduce-scatter.11.cloned.1.call-done = bf16[8,128,128]{2,1,0:T(8,128)(2,1)} async-done(((bf16[128,128,128]{2,1,0:T(8,128)(2,1)}), bf16[8,128,128]{2,1,0:T(8,128)(2,1)}) %reduce-scatter.11.cloned.1.call-update) | async-done | bytes 262160 | tf_op jit(solution)/shard_map/reduce_scatter | solution.py:94
  337.1 42.2 %reduce-scatter.7.cloned.1.call-done = bf16[128,1024]{0,1:T(8,128)(2,1)} async-done(((bf16[128,8192]{0,1:T(8,128)(2,1)}), bf16[128,1024]{0,1:T(8,128)(2,1)}) %reduce-scatter.7.cloned.1.call-update) | async-done | bytes 262160 | tf_op jit(solution)/shard_map/reduce_scatter | solution.py:77
  381.1 41.9 %reduce-scatter.5.cloned.1.call-done = bf16[128,1024]{0,1:T(8,128)(2,1)} async-done(((bf16[128,8192]{0,1:T(8,128)(2,1)}), bf16[128,1024]{0,1:T(8,128)(2,1)}) %reduce-scatter.5.cloned.1.call-update) | async-done | bytes 262160 | tf_op jit(solution)/shard_map/reduce_scatter | solution.py:64
  424.8 45.7 %all-reduce.3.cloned.1.call-done = (bf16[8,128,128]{2,1,0:T(8,128)(2,1)}, bf16[8,128,128]{2,1,0:T(8,128)(2,1)}) async-done(((bf16[8,128,128]{2,1,0:T(8,128)(2,1)}, bf16[8,128,128]{2,1,0:T(8,128)(2,1)}), (bf16[8,128,128]{2,1,0:T(8,128)(2,1)}, bf16[8,128,128]{2,1,0:T(8,128)(2,1)})) %all-reduce.3.cloned.1.call-update) | async-done | bytes 524304 | tf_op jit(solution)/shard_map/psum | solution.py:99
  (62 shorter events, 52.5 us)
Async XLA Ops:
  7.2 10.9 %copy-start = (s32[128,1]{0,1:T(1,128)S(1)}, s32[128,1]{0,1:T(1,128)}, u32[]{:S(2)}) copy-start(s32[128,1]{0,1:T(1,128)} %param.12) | copy-start | bytes 1540
  7.2 44.9 %all-gather.9.cloned.1.call-start = ((), (), s32[]{:S(2)}) async-start(), calls=%async_computation.6 | async-start | bytes 2359296 | tf_op jit(solution)/shard_map/all_gather | solution.py:49
  9.0 85.3 %all-gather.11.cloned.1.call-start = ((), (), s32[]{:S(2)}) async-start(), calls=%async_computation.8 | async-start | bytes 2359296 | tf_op jit(solution)/shard_map/all_gather | solution.py:67
  10.9 127.8 %all-gather.7.cloned.1.call-start = ((), (), s32[]{:S(2)}) async-start(), calls=%async_computation.5 | async-start | bytes 4456448 | tf_op jit(solution)/shard_map/all_gather | solution.py:51
  11.7 168.8 %all-gather.5.cloned.1.call-start = ((), (), s32[]{:S(2)}) async-start(), calls=%async_computation.4 | async-start | bytes 4456448 | tf_op jit(solution)/shard_map/all_gather | solution.py:58
  12.2 308.5 %reduce-scatter.9.cloned.1.call-start = ((), (), s32[]{:S(2)}) async-start(), calls=%async_computation.10 | async-start | bytes 4456448 | tf_op jit(solution)/shard_map/reduce_scatter | solution.py:91
  185.7 5.0 %copy-start.2 = (bf16[128,128,128]{2,1,0:T(8,128)(2,1)S(1)}, bf16[128,128,128]{2,1,0:T(8,128)(2,1)}, u32[]{:S(2)}) copy-start(bf16[128,128,128]{2,1,0:T(8,128)(2,1)} %gather_fusion.4) | copy-start | bytes 12582916
  199.2 137.9 %reduce-scatter.11.cloned.1.call-start = ((), (), s32[]{:S(2)}) async-start(), calls=%async_computation.11 | async-start | bytes 4456448 | tf_op jit(solution)/shard_map/reduce_scatter | solution.py:94
  219.4 160.0 %reduce-scatter.7.cloned.1.call-start = ((), (), s32[]{:S(2)}) async-start(), calls=%async_computation.9 | async-start | bytes 2359296 | tf_op jit(solution)/shard_map/reduce_scatter | solution.py:77
  269.9 153.1 %reduce-scatter.5.cloned.1.call-start = ((), (), s32[]{:S(2)}) async-start(), calls=%async_computation.7 | async-start | bytes 2359296 | tf_op jit(solution)/shard_map/reduce_scatter | solution.py:64
  315.1 158.9 %copy-start.1 = (s32[128,1]{0,1:T(1,128)S(1)}, s32[128,1]{0,1:T(1,128)}, u32[]{:S(2)}) copy-start(s32[128,1]{0,1:T(1,128)} %param.12) | copy-start | bytes 1540
  320.7 149.9 %all-reduce.3.cloned.1.call-start = ((), (), s32[]{:S(2)}) async-start(), calls=%async_computation.12 | async-start | bytes 1048576 | tf_op jit(solution)/shard_map/psum | solution.py:99
Sparse Core Ops, SparseCore 0:
  10.4 41.6 all-gather.8
  54.5 39.8 all-gather.10
  96.2 42.5 all-gather.6
  140.4 39.9 all-gather.4
  199.3 66.5 reduce-scatter.8
  268.4 68.6 reduce-scatter.10
  339.7 39.6 reduce-scatter.6
  381.9 41.0 reduce-scatter.4
  425.7 44.8 all-reduce.2
where the time goes:
time: 482 us; the launch traced here: 481 us
  waiting for transfers between devices  279 us (58%)
  local copies, waits for them, and re-layouts  81.1 us (17%)
  other arithmetic  73.8 us (15%)
  matrix products  32.2 us (7%)
  between operations  14 us (3%)
    scatter-add x2, other arithmetic, add_far(): jnp.zeros((rows_here, model_blocks, block_size), jnp.float32)  53.6 us
    psum x1, waiting for transfers between devices, body(): lax.psum(up_part.astype(jnp.bfloat16), 'dp').astype(jnp.float32)  45.7 us
    reduce_scatter x1, waiting for transfers between devices, body(): lax.psum_scatter(partial_in.astype(jnp.bfloat16), 'tensor', scatter_dimen...  42.2 us
    reduce_scatter x1, waiting for transfers between devices, body(): lax.psum_scatter(partial_out.astype(jnp.bfloat16), 'tensor', scatter_dime...  41.9 us
    all_gather x1, waiting for transfers between devices, body(): full_cotangent = lax.all_gather(cotangent, 'tensor', axis=1, tiled=True)  39 us
    all_gather x1, waiting for transfers between devices, body(): up_whole = lax.all_gather(up_tiles, 'fsdp', axis=0, tiled=True)  32.7 us
    all_gather x1, waiting for transfers between devices, body(): down_whole = lax.all_gather(down_tiles, 'fsdp', axis=0, tiled=True)  31.7 us
    all_gather x1, waiting for transfers between devices, body(): full_input = lax.all_gather(activations, 'tensor', axis=1, tiled=True)  28 us
  transfers between devices with their start and end apart: 9, of which 8 were waited for; matrix products, arithmetic and copies ran while one was open for 34% of the time, Pallas kernels for 0%

commit v1 on v0

--- a/solution.py
+++ b/solution.py
@@ -7,6 +7,19 @@
 FF = 16384
 inv_root_two = 0.7071067811865476
 inv_root_tau = 0.3989422804014327
+
+
+def ring_gather(x, axis, dim):
+    ways = lax.axis_size(axis)
+    up = [(d, (d + 1) % ways) for d in range(ways)]
+    down = [(d, (d - 1) % ways) for d in range(ways)]
+    earlier, later = ([x], [x])
+    for _ in range(ways // 2):
+        earlier.append(lax.ppermute(earlier[-1], axis, up))
+    for _ in range((ways - 1) // 2):
+        later.append(lax.ppermute(later[-1], axis, down))
+    line = jnp.concatenate([*earlier[::-1], *later[1:]], axis=dim)
+    return jnp.roll(line, (lax.axis_index(axis) - ways // 2) * x.shape[dim], axis=dim)
 
 
 def gelu_parts(values):
@@ -46,7 +59,7 @@
     down_back = jnp.argsort(down_order)
     up_far = up_rows[:, 0][up_order]
     down_far = down_cols[:, 0][down_order]
-    full_input = lax.all_gather(activations, "tensor", axis=1, tiled=True)
+    full_input = ring_gather(activations, "tensor", 1)
     input_pick = grouped_pick(full_input, up_far, hidden_blocks, block_size)
     up_whole = lax.all_gather(up_tiles, "fsdp", axis=0, tiled=True)
     up_sorted = grouped_tiles(up_whole, up_order, hidden_blocks)

time: 482 us -> 449 us (0.932)
  waiting for transfers between devices: 279 us -> 234 us
  starting transfers between devices: 0.55 us -> 13.3 us
    all_gather x1, waiting for transfers between devices: 39 us -> 0.01 us  [body(): full_cotangent = lax.all_gather(cotangent, 'tensor', axis=1, tiled=True)]
    all_gather x1 -> x0, waiting for transfers between devices: 28 us -> none  [body(): full_input = lax.all_gather(activations, 'tensor', axis=1, tiled=True)]
    ppermute x0 -> x7, waiting for transfers between devices: none -> 24.4 us  [the longest x4 23.7 us: ring_gather(): earlier.append(lax.ppermute(earlier[-1], axis, up))]
    ppermute x0 -> x7, starting transfers between devices: none -> 12.7 us  [the longest x3 10.2 us: ring_gather(): later.append(lax.ppermute(later[-1], axis, down))]
    all_gather x1, waiting for transfers between devices: 32.7 us -> 27.5 us  [body(): up_whole = lax.all_gather(up_tiles, 'fsdp', axis=0, tiled=True)]
  transfers between devices with their start and end apart: 9 -> 15, of which waited for: 8 -> 11; matrix products, arithmetic and copies ran while one was open for 34% -> 36% of each run, Pallas kernels for 0% -> 0%
where the time goes in v1:
time: 449 us; the launch traced here: 448 us
  waiting for transfers between devices  234 us (52%)
  local copies, waits for them, and re-layouts  79.9 us (18%)
  other arithmetic  73.9 us (16%)
  matrix products  32.2 us (7%)
  between operations  14.5 us (3%)
  starting transfers between devices  13.3 us (3%)
    scatter-add x2, other arithmetic, add_far(): jnp.zeros((rows_here, model_blocks, block_size), jnp.float32)  53.6 us
    psum x1, waiting for transfers between devices, body(): lax.psum(up_part.astype(jnp.bfloat16), 'dp').astype(jnp.float32)  45.9 us
    reduce_scatter x1, waiting for transfers between devices, body(): lax.psum_scatter(partial_in.astype(jnp.bfloat16), 'tensor', scatter_dimen...  42 us
    reduce_scatter x1, waiting for transfers between devices, body(): lax.psum_scatter(partial_out.astype(jnp.bfloat16), 'tensor', scatter_dime...  41.8 us
    all_gather x1, waiting for transfers between devices, body(): down_whole = lax.all_gather(down_tiles, 'fsdp', axis=0, tiled=True)  31.9 us
    all_gather x1, waiting for transfers between devices, body(): up_whole = lax.all_gather(up_tiles, 'fsdp', axis=0, tiled=True)  27.5 us
    ppermute x4, waiting for transfers between devices, ring_gather(): earlier.append(lax.ppermute(earlier[-1], axis, up))  23.7 us
    reduce_scatter x1, waiting for transfers between devices, body(): lax.psum_scatter(down_term.astype(jnp.bfloat16), 'fsdp', scatter_dimensio...  18.9 us
  transfers between devices with their start and end apart: 15, of which 11 were waited for; matrix products, arithmetic and copies ran while one was open for 36% of the time, Pallas kernels for 0%

profile of v1, /device:TPU:1, one launch (start us, length us, event | category | flops | bytes accessed | tf_op | source)
XLA Modules:
  0.0 447.6 jit_solution(830618756637810013)
XLA Ops:
  14.2 4.0 collective-permute-start.4
  30.1 6.4 %collective-permute-done.1 = bf16[128,1024]{0,1:T(8,128)(2,1)S(1)} collective-permute-done((bf16[128,1024]{0,1:T(8,128)(2,1)S(1)}, bf16[128,1024]{0,1:T(8,128)(2,1)S(1)}, u32[]{:S(2)}, u32[]{:S(2)}) %collective-permute-start.1) | collective-permute-done | bytes 262176 | tf_op jit(solution)/shard_map/ppermute | solution.py:18
  41.7 7.9 %collective-permute-done.2 = bf16[128,1024]{0,1:T(8,128)(2,1)S(1)} collective-permute-done((bf16[128,1024]{0,1:T(8,128)(2,1)S(1)}, bf16[128,1024]{0,1:T(8,128)(2,1)S(1)}, u32[]{:S(2)}, u32[]{:S(2)}) %collective-permute-start.2) | collective-permute-done | bytes 262176 | tf_op jit(solution)/shard_map/ppermute | solution.py:18
  53.9 9.3 %collective-permute-done.3 = bf16[128,1024]{0,1:T(8,128)(2,1)S(1)} collective-permute-done((bf16[128,1024]{0,1:T(8,128)(2,1)S(1)}, bf16[128,1024]{0,1:T(8,128)(2,1)S(1)}, u32[]{:S(2)}, u32[]{:S(2)}) %collective-permute-start.3) | collective-permute-done | bytes 262176 | tf_op jit(solution)/shard_map/ppermute | solution.py:18
  77.9 27.5 %all-gather.6.cloned.1.call-done = bf16[128,128,128]{2,1,0:T(8,128)(2,1)} async-done(((bf16[8,128,128]{2,1,0:T(8,128)(2,1)}), bf16[128,128,128]{2,1,0:T(8,128)(2,1)}) %all-gather.6.cloned.1.call-update) | async-done | bytes 4194320 | tf_op jit(solution)/shard_map/all_gather | solution.py:64
  105.3 5.2 %gather_fusion.2 = bf16[128,128,128]{2,1,0:T(8,128)(2,1)} fusion(bf16[128,128,128]{2,1,0:T(8,128)(2,1)} %all-gather.6.cloned.1.call-done, s32[1024]{0:T(1024)S(1)} %pad_clamp_fusion.4), kind=kCustom, calls=%fused_computation.2 | custom fusion | bytes 8389120 | tf_op jit(solution)/shard_map/gather | solution.py:49
  110.5 4.8 %convolution_bitcast_fusion.1 = f32[128,16,128]{0,2,1:T(8,128)S(1)} fusion(bf16[16,8,128,128]{3,2,1,0:T(8,128)(2,1)} %bitcast.76, bf16[128,16,8,128]{3,0,2,1:T(8,128)(2,1)} %bitcast.78), kind=kOutput, calls=%fused_computation.14 | convolution fusion | flops 536870912 | bytes 9437184 | tf_op jit(solution)/shard_map/thkb,hkbc->thc/dot_general | solution.py:66
  115.3 31.9 %all-gather.4.cloned.1.call-done = bf16[128,128,128]{2,1,0:T(8,128)(2,1)} async-done(((bf16[8,128,128]{2,1,0:T(8,128)(2,1)}), bf16[128,128,128]{2,1,0:T(8,128)(2,1)}) %all-gather.4.cloned.1.call-update) | async-done | bytes 4194320 | tf_op jit(solution)/shard_map/all_gather | solution.py:71
  147.2 5.2 %gather_fusion.1 = bf16[128,128,128]{2,1,0:T(8,128)(2,1)} fusion(bf16[128,128,128]{2,1,0:T(8,128)(2,1)} %all-gather.4.cloned.1.call-done, s32[1024]{0:T(1024)S(1)} %pad_clamp_fusion.5), kind=kCustom, calls=%fused_computation.1 | custom fusion | bytes 8389120 | tf_op jit(solution)/shard_map/gather | solution.py:49
  152.5 5.0 %fusion.2 = bf16[128,16,128,1]{0,2,3,1:T(8,128)(2,1)S(1)} fusion(bf16[16,8,128,128]{3,2,1,0:T(8,128)(2,1)} %bitcast.84, bf16[128,16,8,128]{3,0,2,1:T(8,128)(2,1)} %bitcast.86, f32[128,16,128]{0,2,1:T(8,128)S(1)} %convolution_bitcast_fusion.1), kind=kOutput, calls=%fused_computation.17 | convolution fusion | flops 539492352 | bytes 9961472 | tf_op jit(solution)/shard_map/thkc,hkbc->thb/dot_general | solution.py:82
  160.8 5.2 %gather_fusion.6 = bf16[128,128,128]{2,1,0:T(8,128)(2,1)} fusion(bf16[128,128,128]{2,1,0:T(8,128)(2,1)} %bitcast.88, s32[1024]{0:T(1024)S(1)} %get-tuple-element.27), kind=kCustom, calls=%fused_computation.6 | custom fusion | bytes 8389120 | tf_op jit(solution)/shard_map/gather | solution.py:101
  166.0 5.6 %convolution_convert_fusion = bf16[16,8,128,128]{3,2,1,0:T(8,128)(2,1)} fusion(bf16[128,16,8,128]{3,0,2,1:T(8,128)(2,1)} %bitcast.87, f32[128,16,128]{0,2,1:T(8,128)S(1)} %convolution_bitcast_fusion.1), kind=kOutput, calls=%fused_computation.10 | convolution fusion | flops 540278784 | bytes 9437184 | tf_op jit(solution)/shard_map/thb,thkc->hkbc/dot_general | solution.py:96
  171.7 6.4 %copy.79 = bf16[128,128,128]{2,1,0:T(8,128)(2,1)} copy(bf16[128,128,128]{1,2,0:T(8,128)(2,1)} %bitcast.89) | data formatting | bytes 8388608 | tf_op jit(solution)/shard_map/reshape | solution.py:100
  178.0 5.2 %gather_fusion.7 = bf16[128,128,128]{2,1,0:T(8,128)(2,1)} fusion(bf16[128,128,128]{2,1,0:T(8,128)(2,1)} %copy.79, s32[1024]{0:T(1024)S(1)} %get-tuple-element.26), kind=kCustom, calls=%fused_computation.7 | custom fusion | bytes 8389120 | tf_op jit(solution)/shard_map/gather | solution.py:102
  183.6 6.7 %fusion.13 = f32[16,8,128,128]{3,2,1,0:T(8,128)} fusion(bf16[16,8,128,128]{3,2,1,0:T(8,128)(2,1)} %bitcast.77, bf16[128,16,128,1]{0,2,3,1:T(8,128)(2,1)S(1)} %fusion.2), kind=kOutput, calls=%fused_computation.57 | convolution fusion | flops 536870912 | bytes 13107200 | tf_op jit(solution)/shard_map/thc,hkbc->thkb/dot_general | solution.py:86
  190.3 9.0 %copy.73 = f32[128,128,128]{2,0,1:T(8,128)} copy(f32[128,128,128]{0,2,1:T(8,128)} %bitcast.82) | data formatting | bytes 16777216 | tf_op jit(solution)/shard_map/reshape | solution.py:40
  201.8 26.7 %scatter_fusion.1 = f32[128,64,128]{2,0,1:T(8,128)} fusion(f32[128,64,128]{2,0,1:T(8,128)} %broadcast.43.clone.1, s32[128]{0:T(128)S(1)} %fusion.9, f32[128,128,128]{2,1,0:T(8,128)} %bitcast.81), kind=kCustom, calls=%fused_computation.9 | custom fusion | flops 2097152 | bytes 25166336 | tf_op jit(solution)/shard_map/scatter-add | solution.py:42
  234.1 6.8 %fusion.11 = f32[16,8,128,128]{3,2,1,0:T(8,128)} fusion(bf16[16,8,128,128]{3,2,1,0:T(8,128)(2,1)} %bitcast.85, f32[128,16,128]{0,2,1:T(8,128)S(1)} %convolution_bitcast_fusion.1), kind=kOutput, calls=%fused_computation.56 | convolution fusion | flops 538181632 | bytes 13631488 | tf_op jit(solution)/shard_map/thb,hkbc->thkc/dot_general | solution.py:73
  240.9 9.0 %copy.68 = f32[128,128,128]{2,0,1:T(8,128)} copy(f32[128,128,128]{0,2,1:T(8,128)} %bitcast.83) | data formatting | bytes 16777216 | tf_op jit(solution)/shard_map/reshape | solution.py:40
  252.4 26.9 %scatter_fusion = f32[128,64,128]{2,0,1:T(8,128)} fusion(f32[128,64,128]{2,0,1:T(8,128)} %broadcast.43.clone, s32[128]{0:T(128)S(1)} %fusion.8, f32[128,128,128]{2,1,0:T(8,128)} %bitcast.80), kind=kCustom, calls=%fused_computation.8 | custom fusion | flops 2097152 | bytes 25166336 | tf_op jit(solution)/shard_map/scatter-add | solution.py:42
  284.9 18.9 %reduce-scatter.11.cloned.1.call-done = bf16[8,128,128]{2,1,0:T(8,128)(2,1)} async-done(((bf16[128,128,128]{2,1,0:T(8,128)(2,1)}), bf16[8,128,128]{2,1,0:T(8,128)(2,1)}) %reduce-scatter.11.cloned.1.call-update) | async-done | bytes 262160 | tf_op jit(solution)/shard_map/reduce_scatter | solution.py:107
  303.9 42.0 %reduce-scatter.7.cloned.1.call-done = bf16[128,1024]{0,1:T(8,128)(2,1)} async-done(((bf16[128,8192]{0,1:T(8,128)(2,1)}), bf16[128,1024]{0,1:T(8,128)(2,1)}) %reduce-scatter.7.cloned.1.call-update) | async-done | bytes 262160 | tf_op jit(solution)/shard_map/reduce_scatter | solution.py:90
  347.7 41.8 %reduce-scatter.5.cloned.1.call-done = bf16[128,1024]{0,1:T(8,128)(2,1)} async-done(((bf16[128,8192]{0,1:T(8,128)(2,1)}), bf16[128,1024]{0,1:T(8,128)(2,1)}) %reduce-scatter.5.cloned.1.call-update) | async-done | bytes 262160 | tf_op jit(solution)/shard_map/reduce_scatter | solution.py:77
  391.3 45.9 %all-reduce.3.cloned.1.call-done = (bf16[8,128,128]{2,1,0:T(8,128)(2,1)}, bf16[8,128,128]{2,1,0:T(8,128)(2,1)}) async-done(((bf16[8,128,128]{2,1,0:T(8,128)(2,1)}, bf16[8,128,128]{2,1,0:T(8,128)(2,1)}), (bf16[8,128,128]{2,1,0:T(8,128)(2,1)}, bf16[8,128,128]{2,1,0:T(8,128)(2,1)})) %all-reduce.3.cloned.1.call-update) | async-done | bytes 524304 | tf_op jit(solution)/shard_map/psum | solution.py:112
  (89 shorter events, 69.8 us)
Async XLA Ops:
  7.2 14.3 %copy-start = (s32[128,1]{0,1:T(1,128)S(1)}, s32[128,1]{0,1:T(1,128)}, u32[]{:S(2)}) copy-start(s32[128,1]{0,1:T(1,128)} %param.12) | copy-start | bytes 1540
  7.2 64.4 %all-gather.8.cloned.1.call-start = ((), (), s32[]{:S(2)}) async-start(), calls=%async_computation.7 | async-start | bytes 2359296 | tf_op jit(solution)/shard_map/all_gather | solution.py:80
  9.0 96.3 %all-gather.6.cloned.1.call-start = ((), (), s32[]{:S(2)}) async-start(), calls=%async_computation.5 | async-start | bytes 4456448 | tf_op jit(solution)/shard_map/all_gather | solution.py:64
  9.8 137.4 %all-gather.4.cloned.1.call-start = ((), (), s32[]{:S(2)}) async-start(), calls=%async_computation.4 | async-start | bytes 4456448 | tf_op jit(solution)/shard_map/all_gather | solution.py:71
  10.5 274.4 %reduce-scatter.9.cloned.1.call-start = ((), (), s32[]{:S(2)}) async-start(), calls=%async_computation.9 | async-start | bytes 4456448 | tf_op jit(solution)/shard_map/reduce_scatter | solution.py:104
  11.7 14.2 %collective-permute-start = (bf16[128,1024]{0,1:T(8,128)(2,1)S(1)}, bf16[128,1024]{0,1:T(8,128)(2,1)S(1)}, u32[]{:S(2)}, u32[]{:S(2)}) collective-permute-start(bf16[128,1024]{0,1:T(8,128)(2,1)S(1)} %copy.60), channel_id=1, source_target_pairs={{0,1},{1,2},{2,3},{3,4},{4,5},{5,6},{6,7},{7,0},{8,9},{9,10},{10,1... | collective-permute-start | bytes 786440 | tf_op jit(solution)/shard_map/ppermute | solution.py:18
  14.2 24.8 %collective-permute-start.4 = (bf16[128,1024]{0,1:T(8,128)(2,1)S(1)}, bf16[128,1024]{0,1:T(8,128)(2,1)S(1)}, u32[]{:S(2)}, u32[]{:S(2)}) collective-permute-start(bf16[128,1024]{0,1:T(8,128)(2,1)S(1)} %copy.60), channel_id=1, source_target_pairs={{0,7},{1,0},{2,1},{3,2},{4,3},{5,4},{6,5},{7,6},{8,15},{9,8},{10,9... | collective-permute-start | bytes 786440 | tf_op jit(solution)/shard_map/ppermute | solution.py:20
  25.9 10.6 %collective-permute-start.1 = (bf16[128,1024]{0,1:T(8,128)(2,1)S(1)}, bf16[128,1024]{0,1:T(8,128)(2,1)S(1)}, u32[]{:S(2)}, u32[]{:S(2)}) collective-permute-start(bf16[128,1024]{0,1:T(8,128)(2,1)S(1)} %collective-permute-done), channel_id=1, source_target_pairs={{0,1},{1,2},{2,3},{3,4},{4,5},{5,6},{6,7},{7,0},{8,9},{9,10},{10,1... | collective-permute-start | bytes 786440 | tf_op jit(solution)/shard_map/ppermute | solution.py:18
  36.5 13.1 %collective-permute-start.2 = (bf16[128,1024]{0,1:T(8,128)(2,1)S(1)}, bf16[128,1024]{0,1:T(8,128)(2,1)S(1)}, u32[]{:S(2)}, u32[]{:S(2)}) collective-permute-start(bf16[128,1024]{0,1:T(8,128)(2,1)S(1)} %collective-permute-done.1), channel_id=1, source_target_pairs={{0,1},{1,2},{2,3},{3,4},{4,5},{5,6},{6,7},{7,0},{8,9},{9,10},{10,1... | collective-permute-start | bytes 786440 | tf_op jit(solution)/shard_map/ppermute | solution.py:18
  39.1 11.3 %collective-permute-start.5 = (bf16[128,1024]{0,1:T(8,128)(2,1)S(1)}, bf16[128,1024]{0,1:T(8,128)(2,1)S(1)}, u32[]{:S(2)}, u32[]{:S(2)}) collective-permute-start(bf16[128,1024]{0,1:T(8,128)(2,1)S(1)} %collective-permute-done.4), channel_id=1, source_target_pairs={{0,7},{1,0},{2,1},{3,2},{4,3},{5,4},{6,5},{7,6},{8,15},{9,8},{10,9... | collective-permute-start | bytes 786440 | tf_op jit(solution)/shard_map/ppermute | solution.py:20
  49.7 13.5 %collective-permute-start.3 = (bf16[128,1024]{0,1:T(8,128)(2,1)S(1)}, bf16[128,1024]{0,1:T(8,128)(2,1)S(1)}, u32[]{:S(2)}, u32[]{:S(2)}) collective-permute-start(bf16[128,1024]{0,1:T(8,128)(2,1)S(1)} %collective-permute-done.2), channel_id=1, source_target_pairs={{0,1},{1,2},{2,3},{3,4},{4,5},{5,6},{6,7},{7,0},{8,9},{9,10},{10,1... | collective-permute-start | bytes 786440 | tf_op jit(solution)/shard_map/ppermute | solution.py:18
  50.4 13.2 %collective-permute-start.6 = (bf16[128,1024]{0,1:T(8,128)(2,1)S(1)}, bf16[128,1024]{0,1:T(8,128)(2,1)S(1)}, u32[]{:S(2)}, u32[]{:S(2)}) collective-permute-start(bf16[128,1024]{0,1:T(8,128)(2,1)S(1)} %collective-permute-done.5), channel_id=1, source_target_pairs={{0,7},{1,0},{2,1},{3,2},{4,3},{5,4},{6,5},{7,6},{8,15},{9,8},{10,9... | collective-permute-start | bytes 786440 | tf_op jit(solution)/shard_map/ppermute | solution.py:20
  152.5 5.0 %copy-start.2 = (bf16[128,128,128]{2,1,0:T(8,128)(2,1)S(1)}, bf16[128,128,128]{2,1,0:T(8,128)(2,1)}, u32[]{:S(2)}) copy-start(bf16[128,128,128]{2,1,0:T(8,128)(2,1)} %gather_fusion.4) | copy-start | bytes 12582916
  166.0 137.9 %reduce-scatter.11.cloned.1.call-start = ((), (), s32[]{:S(2)}) async-start(), calls=%async_computation.10 | async-start | bytes 4456448 | tf_op jit(solution)/shard_map/reduce_scatter | solution.py:107
  183.3 162.6 %reduce-scatter.7.cloned.1.call-start = ((), (), s32[]{:S(2)}) async-start(), calls=%async_computation.8 | async-start | bytes 2359296 | tf_op jit(solution)/shard_map/reduce_scatter | solution.py:90
  234.1 155.4 %reduce-scatter.5.cloned.1.call-start = ((), (), s32[]{:S(2)}) async-start(), calls=%async_computation.6 | async-start | bytes 2359296 | tf_op jit(solution)/shard_map/reduce_scatter | solution.py:77
  279.3 161.5 %copy-start.1 = (s32[128,1]{0,1:T(1,128)S(1)}, s32[128,1]{0,1:T(1,128)}, u32[]{:S(2)}) copy-start(s32[128,1]{0,1:T(1,128)} %param.12) | copy-start | bytes 1540
  284.9 152.3 %all-reduce.3.cloned.1.call-start = ((), (), s32[]{:S(2)}) async-start(), calls=%async_computation.11 | async-start | bytes 1048576 | tf_op jit(solution)/shard_map/psum | solution.py:112
Sparse Core Ops, SparseCore 0:
  10.4 54.4 all-gather.7
  66.7 38.6 all-gather.5
  107.2 39.9 all-gather.3
  166.1 66.5 reduce-scatter.8
  235.2 68.6 reduce-scatter.10
  306.3 39.5 reduce-scatter.6
  348.4 40.9 reduce-scatter.4
  392.1 45.0 all-reduce.2
